TPU v7x, 32 devices: a whole 2x2x4 slice. The times are simulated.
32 devices in a mesh: wide: 8 (over z, y), narrow: 4 (over x, core).
Axes of the slice: x: 2, y: 2, z: 4, core: 2. Of those that a mesh axis runs over, the one named last changes fastest.
Arguments:
- frames: bfloat16 [256, 2, 256, 256], P(('wide', 'narrow')), may hold values from -120 to 120
- sketch: bfloat16 [256, 128], replicated, may hold values from -0.3 to 2.3
- kernel_taps: bfloat16 [64], replicated, may hold values from -0.3 to 1.1
Outputs:
- basis: float32 [128, 32768], P(None, ('wide', 'narrow'))
- factor: float32 [128, 128], replicated
All inputs are finite; a program needn't handle non-finite values.
Results may differ from a plain program's by a relative error of at most 0.0043.
Values may be sent and summed in bfloat16 or wider, within the bound.
No kernel may reach another device: no remote copies, remote signals or barrier semaphores. Data moves between devices by JAX's collectives and lax.ppermute only.
A program may use at most 64 MiB of HBM per device.

v0:
```python
import jax
import jax.numpy as jnp
from jax import lax
from jax.sharding import PartitionSpec as P


def gauss_taps(spread):
    position = jnp.arange(15, dtype=jnp.float32) - 7.0
    weights = jnp.exp(-position * position / (2.0 * spread * spread))
    return weights / jnp.sum(weights)


def band_matrix(spread, length):
    outputs = length // 2
    offset_index = (
        jnp.arange(length, dtype=jnp.int32)[None, :]
        - 2 * jnp.arange(outputs, dtype=jnp.int32)[:, None]
        + 7
    )
    weights = gauss_taps(spread)
    matrix = jnp.zeros((outputs, length), jnp.float32)
    for offset in range(15):
        matrix = matrix + jnp.where(offset_index == offset, weights[offset], jnp.float32(0.0))
    return matrix


def filter_volumes(frames_block):
    volume = frames_block.astype(jnp.float32)
    row_count = volume.shape[-2]
    col_count = volume.shape[-1]
    half = col_count // 2
    column_bands = jnp.concatenate(
        [band_matrix(1.5, col_count), band_matrix(3.0, col_count)], axis=0
    )
    column_pass = jnp.einsum(
        "...rc,oc->...ro", volume, column_bands, precision=lax.Precision.HIGHEST
    )
    narrow_pass = jnp.einsum(
        "or,...rc->...oc",
        band_matrix(1.5, row_count),
        column_pass[..., :half],
        precision=lax.Precision.HIGHEST,
    )
    broad_pass = jnp.einsum(
        "or,...rc->...oc",
        band_matrix(3.0, row_count),
        column_pass[..., half:],
        precision=lax.Precision.HIGHEST,
    )
    return (narrow_pass - broad_pass).astype(jnp.bfloat16)


def build_toeplitz(kernel_taps, length):
    lag_index = (
        jnp.arange(length, dtype=jnp.int32)[:, None] - jnp.arange(length, dtype=jnp.int32)[None, :]
    )
    toeplitz = jnp.zeros((length, length), jnp.float32)
    for offset in range(kernel_taps.shape[0]):
        toeplitz = toeplitz + jnp.where(
            lag_index == offset, kernel_taps[offset].astype(jnp.float32), jnp.float32(0.0)
        )
    return toeplitz.astype(jnp.bfloat16)


def high_dot(left, right):
    return jnp.dot(left, right, precision=lax.Precision.HIGHEST, preferred_element_type=jnp.float32)


def shards(frames, sketch, kernel_taps):
    filtered = filter_volumes(frames)
    per_device = frames.shape[0]
    flattened = filtered.reshape(per_device, -1)
    voxel_count = flattened.shape[1]
    group_size = lax.axis_size(("wide", "narrow"))
    block = voxel_count // group_size
    length = per_device * group_size
    toeplitz = build_toeplitz(kernel_taps, length)
    arranged = flattened.reshape(1, per_device, group_size, block)
    received = lax.all_to_all(arranged, ("wide", "narrow"), split_axis=2, concat_axis=0, tiled=True)
    deconvolved = jnp.dot(
        toeplitz, received.reshape(length, received.shape[3]), preferred_element_type=jnp.float32
    ).astype(jnp.bfloat16)
    sketched = lax.dot_general(
        sketch, deconvolved, (((0,), (0,)), ((), ())), preferred_element_type=jnp.float32
    )
    deconvolved, sketched = (deconvolved, sketched)
    series = deconvolved.astype(jnp.float32)
    local_gram = (
        lax.dot_general(
            deconvolved, deconvolved, (((1,), (1,)), ((), ())), preferred_element_type=jnp.float32
        )
        / voxel_count
    )
    data_gram = lax.psum(local_gram, ("wide", "narrow"))
    sketch_full = sketch.astype(jnp.float32)
    weighted = high_dot(data_gram, sketch_full)
    first_lower = jnp.linalg.cholesky(high_dot(sketch_full.T, weighted))
    projected = jax.scipy.linalg.solve_triangular(first_lower, weighted.T, lower=True).T
    second_lower = jnp.linalg.cholesky(high_dot(projected.T, high_dot(data_gram, projected)))
    combined = jax.scipy.linalg.solve_triangular(second_lower, projected.T, lower=True)
    basis = high_dot(combined, series)
    factor = second_lower.T
    return (basis, factor)


def solution(mesh):
    return jax.shard_map(
        shards,
        mesh=mesh,
        in_specs=(P(("wide", "narrow"), None, None, None), P(), P()),
        out_specs=(P(None, ("wide", "narrow")), P()),
        check_vma=False,
    )
```

profile of v0, /device:TPU:0, one launch (start us, length us, event | category | flops | bytes accessed | tf_op | source)
XLA Modules:
  0.0 296.3 jit_solution(4108505157623894362)
XLA Ops:
  7.2 0.6 fusion.237
  7.8 0.6 fusion.238
  8.4 0.7 broadcast_divide_fusion.1
  9.1 0.7 fusion.341
  9.8 0.7 broadcast_divide_fusion
  10.4 0.7 fusion.342
  11.1 9.6 %select_add_fusion.1 = f32[128,256]{1,0:T(8,128)S(1)} fusion(f32[]{:T(128)} %bitcast.78, f32[]{:T(128)} %bitcast.77, f32[]{:T(128)} %bitcast.76, f32[]{:T(128)} %bitcast.75, f32[]{:T(128)} %bitcast.74, f32[]{:T(128)} %bitcast.73, f32[]{:T(128)} %bitcast.72, f32[]{:T(128)} %bitcast.71, f32[]{:T(128)} %bitcast.70, f32[]{:T(128)} %bitcast.69, f32[]{:T(128)} %bitcast.68, ...), kind=kLoop, calls=%fused_computation.85 | loop fusion | flops 1507328 | bytes 131644 | tf_op jit(solution)/shard_map/add | solution.py:23
  20.7 9.7 %select_add_fusion = f32[128,256]{1,0:T(8,128)S(1)} fusion(f32[]{:T(128)} %bitcast.93, f32[]{:T(128)} %bitcast.92, f32[]{:T(128)} %bitcast.91, f32[]{:T(128)} %bitcast.90, f32[]{:T(128)} %bitcast.89, f32[]{:T(128)} %bitcast.88, f32[]{:T(128)} %bitcast.87, f32[]{:T(128)} %bitcast.86, f32[]{:T(128)} %bitcast.85, f32[]{:T(128)} %bitcast.84, f32[]{:T(128)} %bitcast.83, ...), kind=kLoop, calls=%fused_computation.84 | loop fusion | flops 1507328 | bytes 131644 | tf_op jit(solution)/shard_map/add | solution.py:23
  30.4 1.9 convolution_bitcast_fusion
  32.3 11.5 %fusion = f32[8,2,128,128]{3,2,1,0:T(8,128)S(1)} fusion(f32[8,2,256,256]{2,3,1,0:T(8,128)S(1)} %convolution_bitcast_fusion, f32[]{:T(128)} %bitcast.93, f32[]{:T(128)} %bitcast.92, f32[]{:T(128)} %bitcast.91, f32[]{:T(128)} %bitcast.90, f32[]{:T(128)} %bitcast.89, f32[]{:T(128)} %bitcast.88, f32[]{:T(128)} %bitcast.87, f32[]{:T(128)} %bitcast.86, ...), kind=kOutput, calls=%fused_computation.1 | convolution fusion | flops 806813696 | bytes 3146300 | tf_op jit(solution)/shard_map/or,...rc->...oc/dot_general | solution.py:44
  43.8 11.4 %fusion.10 = bf16[8,2,128,128]{2,3,1,0:T(8,128)(2,1)S(1)} fusion(f32[8,2,128,128]{3,2,1,0:T(8,128)S(1)} %fusion, f32[8,2,256,256]{2,3,1,0:T(8,128)S(1)} %convolution_bitcast_fusion, f32[]{:T(128)} %bitcast.78, f32[]{:T(128)} %bitcast.77, f32[]{:T(128)} %bitcast.76, f32[]{:T(128)} %bitcast.75, f32[]{:T(128)} %bitcast.74, f32[]{:T(128)} %bitcast.73, ...), kind=kOutput, calls=%fused_computation.8 | convolution fusion | flops 807337984 | bytes 3670588 | tf_op jit(solution)/shard_map/or,...rc->...oc/dot_general | solution.py:38
  55.7 1.1 copy.14
  56.8 7.3 %all-to-all-start = ((bf16[1,8,32,1024]{3,1,0,2:T(8,128)(2,1)}), bf16[1,8,32,1024]{3,1,0,2:T(8,128)(2,1)S(1)}, u32[]{:S(2)}, u32[]{:S(2)}) async-start(bf16[1,8,32,1024]{3,1,0,2:T(8,128)(2,1)} %copy.14), calls=%async_computation | async-start | bytes 1048576 | tf_op jit(solution)/shard_map/all_to_all | solution.py:79
  64.4 0.7 fusion.338
  70.2 0.7 fusion.337
  83.5 0.7 fusion.339
  102.4 0.7 fusion.340
  107.5 1.1 convolution_convert_fusion
  108.6 1.0 convolution_multiply_fusion
  109.7 128.0 %all-reduce.2.cloned.1.call-done = f32[256,256]{1,0:T(8,128)} async-done(((f32[256,256]{1,0:T(8,128)}), f32[256,256]{1,0:T(8,128)}) %all-reduce.2.cloned.1.call-update) | async-done | bytes 262160 | tf_op jit(solution)/shard_map/psum | solution.py:94
  237.7 1.2 fusion.343
  239.3 11.7 %cholesky.44 = f32[128,128]{1,0:T(8,128)S(1)} custom-call(f32[128,128]{1,0:T(8,128)S(1)} %add_multiply_fusion), custom_call_target="Cholesky" | custom-call | tf_op jit(solution)/shard_map/jit(cholesky)/cholesky | solution.py:97
  251.1 0.6 compare_reduce_fusion.1
  251.7 0.7 fusion.228
  252.4 9.8 %custom-call.6 = f32[1,128,128]{1,2,0:T(8,128)S(1)} custom-call(f32[1,128,128]{2,1,0:T(8,128)S(1)} %fusion.228), custom_call_target="InvertDiagBlocksLowerTriangular" | custom-call | tf_op jit(solution)/shard_map/jit(_solve_triangular)/triangular_solve | solution.py:98
  262.5 1.3 fusion.345
  264.2 11.9 %cholesky.55 = f32[128,128]{1,0:T(8,128)S(1)} custom-call(f32[128,128]{1,0:T(8,128)S(1)} %fusion.231), custom_call_target="Cholesky" | custom-call | tf_op jit(solution)/shard_map/jit(cholesky)/cholesky | solution.py:99
  276.1 0.6 compare_reduce_fusion
  276.8 0.7 fusion.236
  277.4 9.8 %custom-call.7 = f32[1,128,128]{1,2,0:T(8,128)S(1)} custom-call(f32[1,128,128]{2,1,0:T(8,128)S(1)} %get-tuple-element.11), custom_call_target="InvertDiagBlocksLowerTriangular" | custom-call | tf_op jit(solution)/shard_map/jit(_solve_triangular)/triangular_solve | solution.py:100
  287.6 1.2 fusion.347
  288.7 0.7 copy.17
  (22 shorter events, 2.2 us)
Async XLA Ops:
  7.2 23.2 %copy-start = (bf16[8,2,256,256]{3,2,1,0:T(8,128)(2,1)S(1)}, bf16[8,2,256,256]{3,2,1,0:T(8,128)(2,1)}, u32[]{:S(2)}) copy-start(bf16[8,2,256,256]{3,2,1,0:T(8,128)(2,1)} %param.6) | copy-start | bytes 6291460
  55.2 9.2 %copy-start.1 = (bf16[64]{0:T(256)(128)(2,1)S(1)}, bf16[64]{0:T(256)(128)(2,1)}, u32[]{:S(2)}) copy-start(bf16[64]{0:T(256)(128)(2,1)} %param.8) | copy-start | bytes 388
  56.8 50.7 %all-to-all-start = ((bf16[1,8,32,1024]{3,1,0,2:T(8,128)(2,1)}), bf16[1,8,32,1024]{3,1,0,2:T(8,128)(2,1)S(1)}, u32[]{:S(2)}, u32[]{:S(2)}) async-start(bf16[1,8,32,1024]{3,1,0,2:T(8,128)(2,1)} %copy.14), calls=%async_computation | async-start | bytes 1048576 | tf_op jit(solution)/shard_map/all_to_all | solution.py:79
  64.2 173.5 %all-reduce.2.cloned.1.call-start = ((), (), s32[]{:S(2)}) async-start(), calls=%async_computation.1 | async-start | bytes 524288 | tf_op jit(solution)/shard_map/psum | solution.py:94
  107.5 130.2 %copy-start.2 = (bf16[256,128]{1,0:T(8,128)(2,1)S(1)}, bf16[256,128]{1,0:T(8,128)(2,1)}, u32[]{:S(2)}) copy-start(bf16[256,128]{1,0:T(8,128)(2,1)} %param.7) | copy-start | bytes 196612
Sparse Core Ops, SparseCore 0:
  109.8 127.8 all-reduce.1
where the time goes:
time: 298 us; the launch traced here: 296 us
  waiting for transfers between devices  128 us (43%)
  other arithmetic  67.7 us (23%)
  between operations  54.4 us (18%)
  matrix products  31.8 us (11%)
  starting transfers between devices  7.54 us (3%)
  local copies, waits for them, and re-layouts  6.83 us (2%)
    psum x1, waiting for transfers between devices, shards(): data_gram = lax.psum(local_gram, ('wide', 'narrow'))  128 us
    add x2, other arithmetic, band_matrix(): matrix + jnp.where(offset_index == offset, weights[offset], jnp.float32(0...  19.2 us
    another operation x3, other arithmetic, shards(): jnp.linalg.cholesky(high_dot(projected.T, high_dot(data_gram, projected)))  12.6 us
    another operation x3, other arithmetic, shards(): first_lower = jnp.linalg.cholesky(high_dot(sketch_full.T, weighted))  12.4 us
    dot_general x1, matrix products, filter_volumes(): jnp.einsum('or,...rc->...oc', band_matrix(3.0, row_count), column_pass[.....  11.5 us
    dot_general x1, matrix products, filter_volumes(): jnp.einsum('or,...rc->...oc', band_matrix(1.5, row_count), column_pass[.....  11.4 us
    another operation x2, other arithmetic, shards(): jax.scipy.linalg.solve_triangular(first_lower, weighted.T, lower=True)  10.5 us
    another operation x1, other arithmetic, shards(): jax.scipy.linalg.solve_triangular(second_lower, projected.T, lower=True)  9.81 us
  transfers between devices with their start and end apart: 2, of which 1 were waited for; matrix products, arithmetic and copies ran while one was open for 1% of the time, Pallas kernels for 0%

commit v1 on v0

--- a/solution.py
+++ b/solution.py
@@ -91,7 +91,7 @@
         )
         / voxel_count
     )
-    data_gram = lax.psum(local_gram, ("wide", "narrow"))
+    data_gram = jnp.sum(lax.all_gather(local_gram, ("wide", "narrow")), axis=0)
     sketch_full = sketch.astype(jnp.float32)
     weighted = high_dot(data_gram, sketch_full)
     first_lower = jnp.linalg.cholesky(high_dot(sketch_full.T, weighted))

time: 298 us -> 250 us (0.84)
  waiting for transfers between devices: 128 us -> 78.4 us
  other arithmetic: 67.7 us -> 71.7 us
    psum x1 -> x0, waiting for transfers between devices: 128 us -> none  [shards(): data_gram = lax.psum(local_gram, ('wide', 'narrow'))]
    all_gather x0 -> x1, waiting for transfers between devices: none -> 78.4 us  [shards(): data_gram = jnp.sum(lax.all_gather(local_gram, ('wide', 'narrow')), axis=0)]
    reduce_sum x0 -> x1, other arithmetic: none -> 3.96 us  [shards(): data_gram = jnp.sum(lax.all_gather(local_gram, ('wide', 'narrow')), axis=0)]
where the time goes in v1:
time: 250 us; the launch traced here: 249 us
  waiting for transfers between devices  78.4 us (31%)
  other arithmetic  71.7 us (29%)
  between operations  54.4 us (22%)
  matrix products  30 us (12%)
  starting transfers between devices  7.55 us (3%)
  local copies, waits for them, and re-layouts  6.8 us (3%)
    all_gather x1, waiting for transfers between devices, shards(): data_gram = jnp.sum(lax.all_gather(local_gram, ('wide', 'narrow')), axis=0)  78.4 us
    add x2, other arithmetic, band_matrix(): matrix + jnp.where(offset_index == offset, weights[offset], jnp.float32(0...  19.2 us
    another operation x3, other arithmetic, shards(): jnp.linalg.cholesky(high_dot(projected.T, high_dot(data_gram, projected)))  12.6 us
    another operation x3, other arithmetic, shards(): first_lower = jnp.linalg.cholesky(high_dot(sketch_full.T, weighted))  12.4 us
    dot_general x1, matrix products, filter_volumes(): jnp.einsum('or,...rc->...oc', band_matrix(3.0, row_count), column_pass[.....  11.5 us
    dot_general x1, matrix products, filter_volumes(): jnp.einsum('or,...rc->...oc', band_matrix(1.5, row_count), column_pass[.....  11.4 us
    another operation x2, other arithmetic, shards(): jax.scipy.linalg.solve_triangular(first_lower, weighted.T, lower=True)  10.5 us
    another operation x1, other arithmetic, shards(): jax.scipy.linalg.solve_triangular(second_lower, projected.T, lower=True)  9.81 us
  transfers between devices with their start and end apart: 2, of which 1 were waited for; matrix products, arithmetic and copies ran while one was open for 1% of the time, Pallas kernels for 0%

profile of v1, /device:TPU:0, one launch (start us, length us, event | category | flops | bytes accessed | tf_op | source)
XLA Modules:
  0.0 248.9 jit_solution(8476787075822395015)
XLA Ops:
  7.2 0.6 fusion.238
  7.8 0.6 fusion.237
  8.4 0.7 broadcast_divide_fusion.1
  9.1 0.7 broadcast_divide_fusion
  9.7 0.7 fusion.342
  10.5 0.7 fusion.341
  11.2 9.6 %select_add_fusion.1 = f32[128,256]{1,0:T(8,128)S(1)} fusion(f32[]{:T(128)} %bitcast.78, f32[]{:T(128)} %bitcast.77, f32[]{:T(128)} %bitcast.76, f32[]{:T(128)} %bitcast.75, f32[]{:T(128)} %bitcast.74, f32[]{:T(128)} %bitcast.73, f32[]{:T(128)} %bitcast.72, f32[]{:T(128)} %bitcast.71, f32[]{:T(128)} %bitcast.70, f32[]{:T(128)} %bitcast.69, f32[]{:T(128)} %bitcast.68, ...), kind=kLoop, calls=%fused_computation.85 | loop fusion | flops 1507328 | bytes 131644 | tf_op jit(solution)/shard_map/add | solution.py:23
  20.7 9.7 %select_add_fusion = f32[128,256]{1,0:T(8,128)S(1)} fusion(f32[]{:T(128)} %bitcast.93, f32[]{:T(128)} %bitcast.92, f32[]{:T(128)} %bitcast.91, f32[]{:T(128)} %bitcast.90, f32[]{:T(128)} %bitcast.89, f32[]{:T(128)} %bitcast.88, f32[]{:T(128)} %bitcast.87, f32[]{:T(128)} %bitcast.86, f32[]{:T(128)} %bitcast.85, f32[]{:T(128)} %bitcast.84, f32[]{:T(128)} %bitcast.83, ...), kind=kLoop, calls=%fused_computation.84 | loop fusion | flops 1507328 | bytes 131644 | tf_op jit(solution)/shard_map/add | solution.py:23
  30.4 2.0 convolution_bitcast_fusion
  32.4 11.5 %fusion = f32[8,2,128,128]{3,2,1,0:T(8,128)S(1)} fusion(f32[8,2,256,256]{2,3,1,0:T(8,128)S(1)} %convolution_bitcast_fusion, f32[]{:T(128)} %bitcast.93, f32[]{:T(128)} %bitcast.92, f32[]{:T(128)} %bitcast.91, f32[]{:T(128)} %bitcast.90, f32[]{:T(128)} %bitcast.89, f32[]{:T(128)} %bitcast.88, f32[]{:T(128)} %bitcast.87, f32[]{:T(128)} %bitcast.86, ...), kind=kOutput, calls=%fused_computation.1 | convolution fusion | flops 806813696 | bytes 3146300 | tf_op jit(solution)/shard_map/or,...rc->...oc/dot_general | solution.py:44
  43.9 11.4 %fusion.10 = bf16[8,2,128,128]{2,3,1,0:T(8,128)(2,1)S(1)} fusion(f32[8,2,128,128]{3,2,1,0:T(8,128)S(1)} %fusion, f32[8,2,256,256]{2,3,1,0:T(8,128)S(1)} %convolution_bitcast_fusion, f32[]{:T(128)} %bitcast.78, f32[]{:T(128)} %bitcast.77, f32[]{:T(128)} %bitcast.76, f32[]{:T(128)} %bitcast.75, f32[]{:T(128)} %bitcast.74, f32[]{:T(128)} %bitcast.73, ...), kind=kOutput, calls=%fused_computation.8 | convolution fusion | flops 807337984 | bytes 3670588 | tf_op jit(solution)/shard_map/or,...rc->...oc/dot_general | solution.py:38
  55.9 1.1 copy.14
  57.0 7.3 %all-to-all-start = ((bf16[1,8,32,1024]{3,1,0,2:T(8,128)(2,1)}), bf16[1,8,32,1024]{3,1,0,2:T(8,128)(2,1)S(1)}, u32[]{:S(2)}, u32[]{:S(2)}) async-start(bf16[1,8,32,1024]{3,1,0,2:T(8,128)(2,1)} %copy.14), calls=%async_computation | async-start | bytes 1048576 | tf_op jit(solution)/shard_map/all_to_all | solution.py:79
  64.5 0.7 fusion.340
  69.6 0.7 fusion.338
  82.3 0.7 fusion.337
  94.9 0.7 fusion.339
  107.5 1.1 convolution_convert_fusion
  108.6 1.0 convolution_multiply_fusion
  109.7 78.4 %all-gather.3.cloned.1.call-done = f32[8192,256]{1,0:T(8,128)} async-done(((f32[256,256]{1,0:T(8,128)}), f32[8192,256]{1,0:T(8,128)}) %all-gather.3.cloned.1.call-update) | async-done | bytes 8388624 | tf_op jit(solution)/shard_map/all_gather | solution.py:94
  188.1 4.0 %reduce_sum.29 = f32[256,256]{1,0:T(8,128)S(1)} reduce(f32[32,256,256]{2,1,0:T(8,128)} %bitcast.223, f32[]{:T(128)} %constant.80.clone.1), dimensions={0}, to_apply=%region_2.3 | reduce | flops 2031616 | bytes 8650756 | tf_op jit(solution)/shard_map/reduce_sum | solution.py:94
  192.8 11.7 %cholesky.44 = f32[128,128]{1,0:T(8,128)S(1)} custom-call(f32[128,128]{1,0:T(8,128)S(1)} %add_multiply_fusion), custom_call_target="Cholesky" | custom-call | tf_op jit(solution)/shard_map/jit(cholesky)/cholesky | solution.py:97
  204.5 0.6 compare_reduce_fusion.1
  205.2 0.7 fusion.228
  205.8 9.8 %custom-call.6 = f32[1,128,128]{1,2,0:T(8,128)S(1)} custom-call(f32[1,128,128]{2,1,0:T(8,128)S(1)} %fusion.228), custom_call_target="InvertDiagBlocksLowerTriangular" | custom-call | tf_op jit(solution)/shard_map/jit(_solve_triangular)/triangular_solve | solution.py:98
  216.0 0.4 fusion.345
  216.8 11.9 %cholesky.55 = f32[128,128]{1,0:T(8,128)S(1)} custom-call(f32[128,128]{1,0:T(8,128)S(1)} %fusion.231), custom_call_target="Cholesky" | custom-call | tf_op jit(solution)/shard_map/jit(cholesky)/cholesky | solution.py:99
  228.7 0.6 compare_reduce_fusion
  229.4 0.7 fusion.236
  230.0 0.7 copy.17
  230.8 9.8 %custom-call.7 = f32[1,128,128]{1,2,0:T(8,128)S(1)} custom-call(f32[1,128,128]{2,1,0:T(8,128)S(1)} %get-tuple-element.11), custom_call_target="InvertDiagBlocksLowerTriangular" | custom-call | tf_op jit(solution)/shard_map/jit(_solve_triangular)/triangular_solve | solution.py:100
  240.9 1.2 fusion.347
  (23 shorter events, 2.5 us)
Async XLA Ops:
  7.2 23.2 %copy-start = (bf16[8,2,256,256]{3,2,1,0:T(8,128)(2,1)S(1)}, bf16[8,2,256,256]{3,2,1,0:T(8,128)(2,1)}, u32[]{:S(2)}) copy-start(bf16[8,2,256,256]{3,2,1,0:T(8,128)(2,1)} %param.6) | copy-start | bytes 6291460
  55.3 9.2 %copy-start.1 = (bf16[64]{0:T(256)(128)(2,1)S(1)}, bf16[64]{0:T(256)(128)(2,1)}, u32[]{:S(2)}) copy-start(bf16[64]{0:T(256)(128)(2,1)} %param.8) | copy-start | bytes 388
  57.0 50.6 %all-to-all-start = ((bf16[1,8,32,1024]{3,1,0,2:T(8,128)(2,1)}), bf16[1,8,32,1024]{3,1,0,2:T(8,128)(2,1)S(1)}, u32[]{:S(2)}, u32[]{:S(2)}) async-start(bf16[1,8,32,1024]{3,1,0,2:T(8,128)(2,1)} %copy.14), calls=%async_computation | async-start | bytes 1048576 | tf_op jit(solution)/shard_map/all_to_all | solution.py:79
  64.3 123.8 %all-gather.3.cloned.1.call-start = ((), (), s32[]{:S(2)}) async-start(), calls=%async_computation.1 | async-start | bytes 8650752 | tf_op jit(solution)/shard_map/all_gather | solution.py:94
  188.1 4.0 %copy-start.2 = (bf16[256,128]{1,0:T(8,128)(2,1)S(1)}, bf16[256,128]{1,0:T(8,128)(2,1)}, u32[]{:S(2)}) copy-start(bf16[256,128]{1,0:T(8,128)(2,1)} %param.7) | copy-start | bytes 196612
Sparse Core Ops, SparseCore 0:
  109.8 78.2 all-gather.2
